TPU v7x, 32 devices: a whole 2x2x4 slice. The times are simulated.
32 devices in a mesh: dp: 4 (over z), expert: 8 (over y, x, core).
Axes of the slice: x: 2, y: 2, z: 4, core: 2. Of those that a mesh axis runs over, the one named last changes fastest.
Arguments:
- tokens: bfloat16 [4096, 4096], P(('dp', 'expert')), may hold values from -6 to 6
- expert_ids: int32 [4096, 2], P(('dp', 'expert')), may hold values from 0 to 7, all different within a row; in each aligned block of 128 rows (0 to 127, 128 to 255, ...) at most 36 rows name the same one
- router_probs: float32 [4096, 2], P(('dp', 'expert')), may hold values from 0.1 to 1
- w_gate: bfloat16 [8, 1024, 4096], P('expert', 'dp'), may hold values from -0.09375 to 0.09375
- w_up: bfloat16 [8, 1024, 4096], P('expert', 'dp'), may hold values from -0.09375 to 0.09375
- w_down: bfloat16 [8, 1024, 4096], P('expert', 'dp'), may hold values from -0.1875 to 0.1875
- out_grad: bfloat16 [4096, 4096], P(('dp', 'expert')), may hold values from -6 to 6
Outputs:
- mixed: bfloat16 [4096, 4096], P(('dp', 'expert'))
- input_grad: bfloat16 [4096, 4096], P(('dp', 'expert'))
- prob_grad: float32 [4096, 2], P(('dp', 'expert'))
- grad_gate: bfloat16 [8, 1024, 4096], P('expert', 'dp')
- grad_up: bfloat16 [8, 1024, 4096], P('expert', 'dp')
- grad_down: bfloat16 [8, 1024, 4096], P('expert', 'dp')
Inputs may be any that keep to these rules, and one draw needn't show every extreme that they name: `expert_ids`: each row names 2 different experts. Among the rows of one device no expert is named more than 36 times, a bound that some block reaches.
All inputs are finite; a program needn't handle non-finite values.
Results may differ from a plain program's by a relative error of at most 0.018.
Values may be sent and summed in bfloat16 or wider, within the bound.
A program may use at most 192 MiB of HBM per device.

v0:
```python
import jax
import jax.numpy as jnp
from jax import lax
from jax.sharding import PartitionSpec as P


def deliver(stacked):
    moved_rows = lax.all_to_all(stacked, "expert", split_axis=1, concat_axis=1, tiled=True)
    arrived = lax.all_gather(moved_rows[None], "dp", axis=0, tiled=True)
    return arrived


def send_back(stacked):
    return lax.all_to_all(stacked, "expert", split_axis=1, concat_axis=1, tiled=True)


def on_device(tokens, expert_ids, router_probs, w_gate, w_up, w_down, out_grad):
    tok_rows, model_width = tokens.shape
    top_count = expert_ids.shape[1]
    local_experts = w_gate.shape[0]
    n_expert = lax.axis_size("expert")
    n_replica = lax.axis_size("dp")
    experts = local_experts * n_expert
    slot_depth = max(2, tok_rows * top_count * 9 // (8 * experts))
    slot_total = experts * slot_depth
    blocks = n_replica * n_expert
    flat_ids = expert_ids.reshape(-1)
    onehot = (flat_ids[:, None] == jnp.arange(experts, dtype=jnp.int32)[None, :]).astype(jnp.int32)
    earlier = jnp.cumsum(onehot, axis=0) - onehot
    rank_of = jnp.sum(earlier * onehot, axis=1)
    slot_of = flat_ids * slot_depth + rank_of
    selector = (jnp.arange(slot_total, dtype=jnp.int32)[:, None] == slot_of[None, :]).astype(
        jnp.bfloat16
    )
    by_token = jnp.sum(selector.reshape(slot_total, tok_rows, top_count), axis=2)
    send_tokens = jnp.dot(by_token, tokens, preferred_element_type=jnp.float32).astype(jnp.bfloat16)
    send_tokens = send_tokens.reshape(n_expert, local_experts, slot_depth, model_width)
    scaled = (
        router_probs.reshape(-1)[:, None]
        * jnp.repeat(out_grad, top_count, axis=0).astype(jnp.float32)
    ).astype(jnp.bfloat16)
    send_grads = jnp.dot(selector, scaled, preferred_element_type=jnp.float32).astype(jnp.bfloat16)
    send_grads = send_grads.reshape(n_expert, local_experts, slot_depth, model_width)
    block_shape = (blocks, local_experts, slot_depth, model_width)
    rows_in = deliver(send_tokens[None])[:, 0].reshape(block_shape)
    gate_proj = jnp.einsum("sxmd,xfd->sxmf", rows_in, w_gate, preferred_element_type=jnp.float32)
    up_proj = jnp.einsum("sxmd,xfd->sxmf", rows_in, w_up, preferred_element_type=jnp.float32)
    sigmoid_gate = jax.nn.sigmoid(gate_proj)
    activated = gate_proj * sigmoid_gate
    hidden = (activated * up_proj).astype(jnp.bfloat16)
    expert_out = lax.psum_scatter(
        jnp.einsum("sxmf,xfd->sxmd", hidden, w_down, preferred_element_type=jnp.float32).astype(
            jnp.bfloat16
        ),
        "dp",
        scatter_dimension=0,
        tiled=True,
    )
    back_out = send_back(expert_out[None])[0]
    grads_in = deliver(send_grads[None])[:, 0].reshape(block_shape)
    d_hidden = jnp.einsum("sxmd,xfd->sxmf", grads_in, w_down, preferred_element_type=jnp.float32)
    grad_down = jnp.einsum(
        "sxmf,sxmd->xfd", hidden, grads_in, preferred_element_type=jnp.float32
    ).astype(jnp.bfloat16)
    d_gate = (d_hidden * up_proj * sigmoid_gate * (1.0 + gate_proj * (1.0 - sigmoid_gate))).astype(
        jnp.bfloat16
    )
    d_up = (d_hidden * activated).astype(jnp.bfloat16)
    grad_gate = jnp.einsum(
        "sxmf,sxmd->xfd", d_gate, rows_in, preferred_element_type=jnp.float32
    ).astype(jnp.bfloat16)
    grad_up = jnp.einsum(
        "sxmf,sxmd->xfd", d_up, rows_in, preferred_element_type=jnp.float32
    ).astype(jnp.bfloat16)
    total = jnp.einsum("sxmf,xfd->sxmd", d_gate, w_gate, preferred_element_type=jnp.float32)
    expert_dx = lax.psum_scatter(
        (
            total + jnp.einsum("sxmf,xfd->sxmd", d_up, w_up, preferred_element_type=jnp.float32)
        ).astype(jnp.bfloat16),
        "dp",
        scatter_dimension=0,
        tiled=True,
    )
    back_dx = send_back(expert_dx[None])[0]
    out_slots = back_out.reshape(slot_total, model_width)
    dx_slots = back_dx.reshape(slot_total, model_width)
    per_choice = jnp.dot(selector.T, out_slots, preferred_element_type=jnp.float32)
    per_choice = per_choice.reshape(tok_rows, top_count, model_width)
    mixed = jnp.sum(router_probs[:, :, None] * per_choice, axis=1).astype(jnp.bfloat16)
    prob_grad = jnp.sum(out_grad.astype(jnp.float32)[:, None, :] * per_choice, axis=2)
    input_grad = jnp.dot(by_token.T, dx_slots, preferred_element_type=jnp.float32).astype(
        jnp.bfloat16
    )
    return (mixed, input_grad, prob_grad, grad_gate, grad_up, grad_down)


def solution(mesh):
    in_specs = (
        P(("dp", "expert"), None),
        P(("dp", "expert"), None),
        P(("dp", "expert"), None),
        P("expert", "dp", None),
        P("expert", "dp", None),
        P("expert", "dp", None),
        P(("dp", "expert"), None),
    )
    out_specs = (
        P(("dp", "expert"), None),
        P(("dp", "expert"), None),
        P(("dp", "expert"), None),
        P("expert", "dp", None),
        P("expert", "dp", None),
        P("expert", "dp", None),
    )
    return jax.shard_map(
        on_device, mesh=mesh, in_specs=in_specs, out_specs=out_specs, check_vma=False
    )
```

profile of v0, /device:TPU:0, one launch (start us, length us, event | category | flops | bytes accessed | tf_op | source)
XLA Modules:
  0.0 847.3 jit_solution(7481087154159858697)
XLA Ops:
  17.9 37.4 %all_to_all.20 = bf16[1,8,1,36,4096]{4,3,2,0,1:T(8,128)(2,1)S(1)} all-to-all(bf16[1,8,1,36,4096]{4,3,2,0,1:T(8,128)(2,1)} %bitcast.136), channel_id=1, replica_groups=mesh['dp'=4,'expert'=8] {'expert'}, dimensions={1} | all-to-all | bytes 4718592 | tf_op jit(solution)/shard_map/all_to_all | solution.py:8
  63.2 6.5 convert_element_type.98
  69.7 4.8 convolution_convert_fusion
  78.6 35.7 %all_to_all.21 = bf16[1,8,1,36,4096]{4,3,2,0,1:T(8,128)(2,1)S(1)} all-to-all(bf16[1,8,1,36,4096]{4,3,2,0,1:T(8,128)(2,1)} %bitcast.137), channel_id=1, replica_groups=mesh['dp'=4,'expert'=8] {'expert'}, dimensions={1} | all-to-all | bytes 4718592 | tf_op jit(solution)/shard_map/all_to_all | solution.py:8
  117.4 106.8 %all-gather.5.cloned.1.call-done = bf16[4,8,1,36,4096]{4,1,3,2,0:T(8,128)(2,1)} async-done(((bf16[1,8,1,36,4096]{4,1,3,2,0:T(8,128)(2,1)}), bf16[4,8,1,36,4096]{4,1,3,2,0:T(8,128)(2,1)}) %all-gather.5.cloned.1.call-update) | async-done | bytes 9437200 | tf_op jit(solution)/shard_map/all_gather | solution.py:9
  224.2 13.6 %copy.57 = bf16[4,8,1,36,4096]{4,3,1,0,2:T(8,128)(2,1)} copy(bf16[4,8,1,36,4096]{4,1,3,2,0:T(8,128)(2,1)} %all-gather.5.cloned.1.call-done) | data formatting | bytes 18874368 | tf_op jit(solution)/shard_map/all_gather | solution.py:9
  237.8 8.8 %fusion.21 = f32[32,1,36,256]{3,2,0,1:T(8,128)} fusion(bf16[32,36,4096]{2,1,0:T(8,128)(2,1)} %bitcast.128, bf16[1,256,4096]{2,1,0:T(8,128)(2,1)} %param.11), kind=kOutput, calls=%fused_computation.30 | convolution fusion | flops 2415919104 | bytes 12713984 | tf_op jit(solution)/shard_map/sxmd,xfd->sxmf/dot_general | solution.py:47
  246.7 4.3 fusion.18
  251.0 139.8 %all-gather.7.cloned.1.call-done = bf16[4,8,1,36,4096]{4,1,3,2,0:T(8,128)(2,1)} async-done(((bf16[1,8,1,36,4096]{4,1,3,2,0:T(8,128)(2,1)}), bf16[4,8,1,36,4096]{4,1,3,2,0:T(8,128)(2,1)}) %all-gather.7.cloned.1.call-update) | async-done | bytes 9437200 | tf_op jit(solution)/shard_map/all_gather | solution.py:9
  390.8 13.5 %copy.64 = bf16[4,8,1,36,4096]{4,3,1,0,2:T(8,128)(2,1)} copy(bf16[4,8,1,36,4096]{4,1,3,2,0:T(8,128)(2,1)} %all-gather.7.cloned.1.call-done) | data formatting | bytes 18874368 | tf_op jit(solution)/shard_map/all_gather | solution.py:9
  404.2 9.2 %fusion.29 = (bf16[32,36,256]{2,1,0:T(8,128)(2,1)}, bf16[32,1,36,256]{3,2,0,1:T(8,128)(2,1)S(1)}, bf16[32,36,256]{2,1,0:T(8,128)(2,1)S(1)}) fusion(f32[32,1,36,256]{3,2,0,1:T(8,128)} %fusion.18, f32[32,1,36,256]{3,2,0,1:T(8,128)} %fusion.21, bf16[32,36,4096]{2,1,0:T(8,128)(2,1)} %bitcast.134, bf16[1,256,4096]{2,1,0:T(8,128)(2,1)S(1)} %copy-done), kind=kOutput, calls=%fused_computation.38 | convolution fusion | flops 2420342784 | bytes 15663104 | tf_op jit(solution)/shard_map/sxmd,xfd->sxmf/dot_general | solution.py:61
  413.4 8.7 %fusion.13 = f32[32,36,4096]{2,1,0:T(8,128)} fusion(bf16[1,256,4096]{2,1,0:T(8,128)(2,1)S(1)} %copy-done.5, bf16[32,1,36,256]{3,2,0,1:T(8,128)(2,1)S(1)} %get-tuple-element.9), kind=kOutput, calls=%fused_computation.24 | convolution fusion | flops 2415919104 | bytes 21561344 | tf_op jit(solution)/shard_map/sxmf,xfd->sxmd/dot_general | solution.py:75
  422.1 14.6 %fusion = bf16[32,1,36,4096]{3,2,0,1:T(8,128)(2,1)} fusion(f32[32,36,4096]{2,1,0:T(8,128)} %fusion.13, bf16[32,36,256]{2,1,0:T(8,128)(2,1)} %get-tuple-element.8, bf16[1,256,4096]{2,1,0:T(8,128)(2,1)} %param.11), kind=kOutput, calls=%fused_computation.1 | convolution fusion | flops 2425356288 | bytes 30998528 | tf_op jit(solution)/shard_map/sxmf,xfd->sxmd/dot_general | solution.py:78
  436.8 5.9 convert_bitcast_fusion
  442.7 170.4 %reduce-scatter.5.cloned.1.call-done = bf16[8,1,36,4096]{3,2,0,1:T(8,128)(2,1)} async-done(((bf16[32,1,36,4096]{3,2,0,1:T(8,128)(2,1)}), bf16[8,1,36,4096]{3,2,0,1:T(8,128)(2,1)}) %reduce-scatter.5.cloned.1.call-update) | async-done | bytes 2359312 | tf_op jit(solution)/shard_map/reduce_scatter | solution.py:76
  613.2 4.4 all-to-all-start.3
  622.8 171.7 %reduce-scatter.3.cloned.1.call-done = bf16[8,1,36,4096]{3,2,0,1:T(8,128)(2,1)} async-done(((bf16[32,1,36,4096]{3,2,0,1:T(8,128)(2,1)}), bf16[8,1,36,4096]{3,2,0,1:T(8,128)(2,1)}) %reduce-scatter.3.cloned.1.call-update) | async-done | bytes 2359312 | tf_op jit(solution)/shard_map/reduce_scatter | solution.py:51
  794.5 4.6 all-to-all-start.1
  799.2 8.3 fusion.4
  807.4 8.3 fusion.5
  815.7 4.1 fusion.6
  819.8 4.1 reshape_squeeze.9
  831.4 4.1 reshape.153
  835.5 5.1 multiply_reduce_fusion
  (59 shorter events, 38.5 us)
Async XLA Ops:
  7.2 397.1 %copy-start = (bf16[1,256,4096]{2,1,0:T(8,128)(2,1)S(1)}, bf16[1,256,4096]{2,1,0:T(8,128)(2,1)}, u32[]{:S(2)}) copy-start(bf16[1,256,4096]{2,1,0:T(8,128)(2,1)} %param.12) | copy-start | bytes 6291460
  7.2 217.0 %all-gather.5.cloned.1.call-start = ((), (), s32[]{:S(2)}) async-start(), calls=%async_computation.8 | async-start | bytes 11796480 | tf_op jit(solution)/shard_map/all_gather | solution.py:9
  57.9 0.7 copy-start.7
  57.9 1.2 copy-start.2
  57.9 332.8 %all-gather.7.cloned.1.call-start = ((), (), s32[]{:S(2)}) async-start(), calls=%async_computation.9 | async-start | bytes 11796480 | tf_op jit(solution)/shard_map/all_gather | solution.py:9
  117.1 496.1 %reduce-scatter.5.cloned.1.call-start = ((), (), s32[]{:S(2)}) async-start(), calls=%async_computation.7 | async-start | bytes 13107200 | tf_op jit(solution)/shard_map/reduce_scatter | solution.py:76
  237.8 8.9 %copy-start.1 = (bf16[4,8,1,36,4096]{4,3,1,0,2:T(8,128)(2,1)S(1)}, bf16[4,8,1,36,4096]{4,3,1,0,2:T(8,128)(2,1)}, u32[]{:S(2)}) copy-start(bf16[4,8,1,36,4096]{4,3,1,0,2:T(8,128)(2,1)} %copy.57) | copy-start | bytes 28311556
  237.8 8.9 %copy-start.4 = (bf16[1,256,4096]{2,1,0:T(8,128)(2,1)S(1)}, bf16[1,256,4096]{2,1,0:T(8,128)(2,1)}, u32[]{:S(2)}) copy-start(bf16[1,256,4096]{2,1,0:T(8,128)(2,1)} %param.10) | copy-start | bytes 6291460
  404.2 9.2 %copy-start.5 = (bf16[1,256,4096]{2,1,0:T(8,128)(2,1)S(1)}, bf16[1,256,4096]{2,1,0:T(8,128)(2,1)}, u32[]{:S(2)}) copy-start(bf16[1,256,4096]{2,1,0:T(8,128)(2,1)} %param.10) | copy-start | bytes 6291460
  436.8 357.7 %reduce-scatter.3.cloned.1.call-start = ((), (), s32[]{:S(2)}) async-start(), calls=%async_computation.6 | async-start | bytes 13107200 | tf_op jit(solution)/shard_map/reduce_scatter | solution.py:51
  613.2 181.3 %all-to-all-start.3 = ((bf16[1,8,1,36,4096]{4,3,2,0,1:T(8,128)(2,1)}), bf16[1,8,1,36,4096]{4,3,2,0,1:T(8,128)(2,1)}, u32[]{:S(2)}, u32[]{:S(2)}) async-start(bf16[1,8,1,36,4096]{4,3,2,0,1:T(8,128)(2,1)} %bitcast.139), calls=%async_computation.5 | async-start | bytes 5242880 | tf_op jit(solution)/shard_map/all_to_all | solution.py:14
  794.5 36.9 %all-to-all-start.1 = ((bf16[1,8,1,36,4096]{4,3,2,0,1:T(8,128)(2,1)}), bf16[1,8,1,36,4096]{4,3,2,0,1:T(8,128)(2,1)}, u32[]{:S(2)}, u32[]{:S(2)}) async-start(bf16[1,8,1,36,4096]{4,3,2,0,1:T(8,128)(2,1)} %bitcast.138), calls=%async_computation.2 | async-start | bytes 5242880 | tf_op jit(solution)/shard_map/all_to_all | solution.py:14
  799.1 8.3 copy-start.3
  799.1 16.5 %slice-start = ((s8[10485760]{0:T(1024)(128)(4,1)}), s8[4194304]{0:T(1024)(128)(4,1)S(1)}, s32[]{:S(2)}) async-start(s8[10485760]{0:T(1024)(128)(4,1)} %bitcast.131), calls=%async_computation.10 | async-start | bytes 8388608
  799.2 16.5 %slice-start.1 = ((s8[10485760]{0:T(1024)(128)(4,1)}), s8[4194304]{0:T(1024)(128)(4,1)S(1)}, s32[]{:S(2)}) async-start(s8[10485760]{0:T(1024)(128)(4,1)} %bitcast.131), calls=%async_computation.11 | async-start | bytes 8388608
  807.4 8.3 slice-start.2
  827.3 8.2 copy-start.6
Sparse Core Ops, SparseCore 0:
  58.1 166.1 all-gather.4
  225.8 164.9 all-gather.6
  436.9 176.2 reduce-scatter.4
  615.4 179.0 reduce-scatter.2
where the time goes:
time: 854 us; the launch traced here: 847 us
  waiting for transfers between devices  593 us (69%)
  matrix products  88.9 us (10%)
  blocking collectives  73.1 us (9%)
  local copies, waits for them, and re-layouts  63.9 us (7%)
  between operations  14.1 us (2%)
  starting transfers between devices  9.51 us (1%)
    all_gather x2, waiting for transfers between devices, deliver(): arrived = lax.all_gather(moved_rows[None], 'dp', axis=0, tiled=True)  247 us
    reduce_scatter x1, waiting for transfers between devices, on_device(): lax.psum_scatter(jnp.einsum('sxmf,xfd->sxmd', hidden, w_down, preferred_e...  172 us
    reduce_scatter x1, waiting for transfers between devices, on_device(): lax.psum_scatter((total + jnp.einsum('sxmf,xfd->sxmd', d_up, w_up, prefer...  170 us
    all_to_all x2, blocking collectives, deliver(): lax.all_to_all(stacked, 'expert', split_axis=1, concat_axis=1, tiled=True)  73.1 us
    all_gather x2, local copies, waits for them, and re-layouts, deliver(): arrived = lax.all_gather(moved_rows[None], 'dp', axis=0, tiled=True)  27 us
  transfers between devices with their start and end apart: 6, of which 5 were waited for; matrix products, arithmetic and copies ran while one was open for 10% of the time, Pallas kernels for 0%

commit v1 on v0

--- a/solution.py
+++ b/solution.py
@@ -4,9 +4,14 @@
 from jax.sharding import PartitionSpec as P
 
 
+def swapped_in(x, axis, dim):
+    outgoing = jnp.stack([x] * lax.axis_size(axis))
+    return jnp.concatenate(lax.all_to_all(outgoing, axis, 0, 0), axis=dim)
+
+
 def deliver(stacked):
     moved_rows = lax.all_to_all(stacked, "expert", split_axis=1, concat_axis=1, tiled=True)
-    arrived = lax.all_gather(moved_rows[None], "dp", axis=0, tiled=True)
+    arrived = swapped_in(moved_rows[None], "dp", 0)
     return arrived
 
 

time: 854 us -> 993 us (1.16)
  waiting for transfers between devices: 593 us -> 768 us
  blocking collectives: 73.1 us -> 0 us
  starting transfers between devices: 9.51 us -> 31 us
  local copies, waits for them, and re-layouts: 63.9 us -> 78.3 us
    all_to_all x0 -> x4, waiting for transfers between devices: none -> 418 us  [the longest x2 377 us: swapped_in(): return jnp.concatenate(lax.all_to_all(outgoing, axis, 0, 0), axis=dim)]
    all_gather x2 -> x0, waiting for transfers between devices: 247 us -> none  [deliver(): arrived = lax.all_gather(moved_rows[None], 'dp', axis=0, tiled=True)]
    all_to_all x2 -> x0, blocking collectives: 73.1 us -> none  [deliver(): lax.all_to_all(stacked, 'expert', split_axis=1, concat_axis=1, tiled=True)]
    all_gather x2 -> x0, local copies, waits for them, and re-layouts: 27 us -> none  [deliver(): arrived = lax.all_gather(moved_rows[None], 'dp', axis=0, tiled=True)]
    all_to_all x0 -> x2, local copies, waits for them, and re-layouts: none -> 26.2 us  [swapped_in(): return jnp.concatenate(lax.all_to_all(outgoing, axis, 0, 0), axis=dim)]
    all_to_all x0 -> x4, starting transfers between devices: none -> 21.3 us  [the longest x2 11.6 us: swapped_in(): return jnp.concatenate(lax.all_to_all(outgoing, axis, 0, 0), axis=dim)]
    another operation x1 -> x3, local copies, waits for them, and re-layouts: 0.01 us -> 12.9 us  [the longest x2 12.9 us: swapped_in(): outgoing = jnp.stack([x] * lax.axis_size(axis))]
  transfers between devices with their start and end apart: 6 -> 8, of which waited for: 5 -> 7; matrix products, arithmetic and copies ran while one was open for 10% -> 9% of each run, Pallas kernels for 0% -> 0%
where the time goes in v1:
time: 993 us; the launch traced here: 985 us
  waiting for transfers between devices  768 us (77%)
  matrix products  88.1 us (9%)
  local copies, waits for them, and re-layouts  78.3 us (8%)
  starting transfers between devices  31 us (3%)
  between operations  14.5 us (1%)
    all_to_all x2, waiting for transfers between devices, swapped_in(): return jnp.concatenate(lax.all_to_all(outgoing, axis, 0, 0), axis=dim)  377 us
    reduce_scatter x1, waiting for transfers between devices, on_device(): lax.psum_scatter((total + jnp.einsum('sxmf,xfd->sxmd', d_up, w_up, prefer...  173 us
    reduce_scatter x1, waiting for transfers between devices, on_device(): lax.psum_scatter(jnp.einsum('sxmf,xfd->sxmd', hidden, w_down, preferred_e...  172 us
    all_to_all x2, waiting for transfers between devices, deliver(): lax.all_to_all(stacked, 'expert', split_axis=1, concat_axis=1, tiled=True)  41.1 us
    all_to_all x2, local copies, waits for them, and re-layouts, swapped_in(): return jnp.concatenate(lax.all_to_all(outgoing, axis, 0, 0), axis=dim)  26.2 us
  transfers between devices with their start and end apart: 8, of which 7 were waited for; matrix products, arithmetic and copies ran while one was open for 9% of the time, Pallas kernels for 0%

profile of v1, /device:TPU:0, one launch (start us, length us, event | category | flops | bytes accessed | tf_op | source)
XLA Modules:
  0.0 984.6 jit_solution(52300269903384151)
XLA Ops:
  17.8 5.3 all-to-all-start
  27.5 6.1 convert_element_type.98
  42.2 13.3 %all-to-all-done = bf16[1,8,1,36,4096]{4,3,2,0,1:T(8,128)(2,1)} async-done(((bf16[1,8,1,36,4096]{4,3,2,0,1:T(8,128)(2,1)}), bf16[1,8,1,36,4096]{4,3,2,0,1:T(8,128)(2,1)}, u32[]{:S(2)}, u32[]{:S(2)}) %all-to-all-start) | async-done | bytes 2359328 | tf_op jit(solution)/shard_map/all_to_all | solution.py:13
  64.4 27.8 %all-to-all-done.3 = bf16[1,8,1,36,4096]{4,3,2,0,1:T(8,128)(2,1)} async-done(((bf16[1,8,1,36,4096]{4,3,2,0,1:T(8,128)(2,1)}), bf16[1,8,1,36,4096]{4,3,2,0,1:T(8,128)(2,1)}, u32[]{:S(2)}, u32[]{:S(2)}) %all-to-all-start.3) | async-done | bytes 2359328 | tf_op jit(solution)/shard_map/all_to_all | solution.py:13
  92.2 6.5 stack.6
  98.7 5.8 all-to-all-start.1
  104.5 4.5 copy.63
  109.0 199.0 %all-to-all-done.1 = bf16[4,1,1,8,1,36,4096]{6,3,5,4,2,1,0:T(8,128)(2,1)} async-done(((bf16[4,1,1,8,1,36,4096]{6,3,5,4,2,1,0:T(8,128)(2,1)}), bf16[4,1,1,8,1,36,4096]{6,3,5,4,2,1,0:T(8,128)(2,1)}, u32[]{:S(2)}, u32[]{:S(2)}) %all-to-all-start.1) | async-done | bytes 9437216 | tf_op jit(solution)/shard_map/all_to_all | solution.py:9
  308.0 6.4 stack.7
  314.4 5.8 all-to-all-start.4
  320.8 13.1 %copy.57 = bf16[4,1,1,8,1,36,4096]{6,5,3,0,4,2,1:T(8,128)(2,1)} copy(bf16[4,1,1,8,1,36,4096]{6,3,5,4,2,1,0:T(8,128)(2,1)} %all-to-all-done.1) | data formatting | bytes 18874368 | tf_op jit(solution)/shard_map/all_to_all | solution.py:9
  333.8 8.8 fusion.21
  347.0 178.2 %all-to-all-done.4 = bf16[4,1,1,8,1,36,4096]{6,3,5,4,2,1,0:T(8,128)(2,1)} async-done(((bf16[4,1,1,8,1,36,4096]{6,3,5,4,2,1,0:T(8,128)(2,1)}), bf16[4,1,1,8,1,36,4096]{6,3,5,4,2,1,0:T(8,128)(2,1)}, u32[]{:S(2)}, u32[]{:S(2)}) %all-to-all-start.4) | async-done | bytes 9437216 | tf_op jit(solution)/shard_map/all_to_all | solution.py:9
  525.2 13.1 %copy.64 = bf16[4,1,1,8,1,36,4096]{6,5,3,0,4,2,1:T(8,128)(2,1)} copy(bf16[4,1,1,8,1,36,4096]{6,3,5,4,2,1,0:T(8,128)(2,1)} %all-to-all-done.4) | data formatting | bytes 18874368 | tf_op jit(solution)/shard_map/all_to_all | solution.py:9
  538.3 9.2 fusion.29
  547.5 8.8 fusion.13
  556.2 14.6 %fusion = bf16[32,1,36,4096]{3,2,0,1:T(8,128)(2,1)} fusion(f32[32,36,4096]{2,1,0:T(8,128)} %fusion.13, bf16[32,36,256]{2,1,0:T(8,128)(2,1)} %get-tuple-element.8, bf16[1,256,4096]{2,1,0:T(8,128)(2,1)} %param.11), kind=kOutput, calls=%fused_computation.1 | convolution fusion | flops 2425356288 | bytes 30998528 | tf_op jit(solution)/shard_map/sxmf,xfd->sxmd/dot_general | solution.py:83
  570.9 5.5 convert_bitcast_fusion
  576.5 173.4 %reduce-scatter.5.cloned.1.call-done = bf16[8,1,36,4096]{3,2,0,1:T(8,128)(2,1)} async-done(((bf16[32,1,36,4096]{3,2,0,1:T(8,128)(2,1)}), bf16[8,1,36,4096]{3,2,0,1:T(8,128)(2,1)}) %reduce-scatter.5.cloned.1.call-update) | async-done | bytes 2359312 | tf_op jit(solution)/shard_map/reduce_scatter | solution.py:81
  759.5 171.8 %reduce-scatter.3.cloned.1.call-done = bf16[8,1,36,4096]{3,2,0,1:T(8,128)(2,1)} async-done(((bf16[32,1,36,4096]{3,2,0,1:T(8,128)(2,1)}), bf16[8,1,36,4096]{3,2,0,1:T(8,128)(2,1)}) %reduce-scatter.3.cloned.1.call-update) | async-done | bytes 2359312 | tf_op jit(solution)/shard_map/reduce_scatter | solution.py:56
  931.4 4.7 all-to-all-start.2
  936.1 8.3 fusion.4
  944.4 8.3 fusion.5
  972.4 5.1 multiply_reduce_fusion
  (61 shorter events, 66.8 us)
Async XLA Ops:
  7.2 531.1 %copy-start = (bf16[1,256,4096]{2,1,0:T(8,128)(2,1)S(1)}, bf16[1,256,4096]{2,1,0:T(8,128)(2,1)}, u32[]{:S(2)}) copy-start(bf16[1,256,4096]{2,1,0:T(8,128)(2,1)} %param.12) | copy-start | bytes 6291460
  17.8 5.3 copy-start.7
  17.8 5.6 copy-start.2
  17.8 37.7 %all-to-all-start = ((bf16[1,8,1,36,4096]{4,3,2,0,1:T(8,128)(2,1)}), bf16[1,8,1,36,4096]{4,3,2,0,1:T(8,128)(2,1)}, u32[]{:S(2)}, u32[]{:S(2)}) async-start(bf16[1,8,1,36,4096]{4,3,2,0,1:T(8,128)(2,1)} %bitcast.138), calls=%async_computation | async-start | bytes 5242880 | tf_op jit(solution)/shard_map/all_to_all | solution.py:13
  55.5 36.6 %all-to-all-start.3 = ((bf16[1,8,1,36,4096]{4,3,2,0,1:T(8,128)(2,1)}), bf16[1,8,1,36,4096]{4,3,2,0,1:T(8,128)(2,1)}, u32[]{:S(2)}, u32[]{:S(2)}) async-start(bf16[1,8,1,36,4096]{4,3,2,0,1:T(8,128)(2,1)} %bitcast.139), calls=%async_computation.4 | async-start | bytes 5242880 | tf_op jit(solution)/shard_map/all_to_all | solution.py:13
  98.7 209.3 %all-to-all-start.1 = ((bf16[4,1,1,8,1,36,4096]{6,3,5,4,2,1,0:T(8,128)(2,1)}), bf16[4,1,1,8,1,36,4096]{6,3,5,4,2,1,0:T(8,128)(2,1)}, u32[]{:S(2)}, u32[]{:S(2)}) async-start(bf16[4,1,1,8,1,36,4096]{6,3,5,4,2,1,0:T(8,128)(2,1)} %stack.6), calls=%async_computation.1 | async-start | bytes 18874368 | tf_op jit(solution)/shard_map/all_to_all | solution.py:9
  314.4 210.8 %all-to-all-start.4 = ((bf16[4,1,1,8,1,36,4096]{6,3,5,4,2,1,0:T(8,128)(2,1)}), bf16[4,1,1,8,1,36,4096]{6,3,5,4,2,1,0:T(8,128)(2,1)}, u32[]{:S(2)}, u32[]{:S(2)}) async-start(bf16[4,1,1,8,1,36,4096]{6,3,5,4,2,1,0:T(8,128)(2,1)} %stack.7), calls=%async_computation.5 | async-start | bytes 18874368 | tf_op jit(solution)/shard_map/all_to_all | solution.py:9
  320.2 429.7 %reduce-scatter.5.cloned.1.call-start = ((), (), s32[]{:S(2)}) async-start(), calls=%async_computation.9 | async-start | bytes 13107200 | tf_op jit(solution)/shard_map/reduce_scatter | solution.py:81
  333.8 8.8 copy-start.1
  333.8 8.8 copy-start.4
  538.3 9.2 copy-start.5
  570.9 360.5 %reduce-scatter.3.cloned.1.call-start = ((), (), s32[]{:S(2)}) async-start(), calls=%async_computation.8 | async-start | bytes 13107200 | tf_op jit(solution)/shard_map/reduce_scatter | solution.py:56
  749.9 181.5 %all-to-all-start.5 = ((bf16[1,8,1,36,4096]{4,3,2,0,1:T(8,128)(2,1)}), bf16[1,8,1,36,4096]{4,3,2,0,1:T(8,128)(2,1)}, u32[]{:S(2)}, u32[]{:S(2)}) async-start(bf16[1,8,1,36,4096]{4,3,2,0,1:T(8,128)(2,1)} %bitcast.141), calls=%async_computation.7 | async-start | bytes 5242880 | tf_op jit(solution)/shard_map/all_to_all | solution.py:19
  931.4 36.9 %all-to-all-start.2 = ((bf16[1,8,1,36,4096]{4,3,2,0,1:T(8,128)(2,1)}), bf16[1,8,1,36,4096]{4,3,2,0,1:T(8,128)(2,1)}, u32[]{:S(2)}, u32[]{:S(2)}) async-start(bf16[1,8,1,36,4096]{4,3,2,0,1:T(8,128)(2,1)} %bitcast.140), calls=%async_computation.3 | async-start | bytes 5242880 | tf_op jit(solution)/shard_map/all_to_all | solution.py:19
  936.1 8.3 copy-start.3
  936.1 16.5 %slice-start = ((s8[10485760]{0:T(1024)(128)(4,1)}), s8[4194304]{0:T(1024)(128)(4,1)S(1)}, s32[]{:S(2)}) async-start(s8[10485760]{0:T(1024)(128)(4,1)} %bitcast.133), calls=%async_computation.10 | async-start | bytes 8388608
  936.1 16.5 %slice-start.1 = ((s8[10485760]{0:T(1024)(128)(4,1)}), s8[4194304]{0:T(1024)(128)(4,1)S(1)}, s32[]{:S(2)}) async-start(s8[10485760]{0:T(1024)(128)(4,1)} %bitcast.133), calls=%async_computation.11 | async-start | bytes 8388608
  944.4 8.3 slice-start.2
  964.2 8.2 copy-start.6
Sparse Core Ops, SparseCore 0:
  571.0 178.8 reduce-scatter.4
  752.3 179.0 reduce-scatter.2
